TPU v7x, 256 devices: a whole 4x4x8 slice. The times are simulated.
256 devices in a mesh: seq: 64 (over z, x, core), tp: 4 (over y).
Axes of the slice: x: 4, y: 4, z: 8, core: 2. Of those that a mesh axis runs over, the one named last changes fastest.
Arguments:
- layer_input: bfloat16 [16384, 2048], P('seq'), may hold values from -1.5 to 1.5
- norm_gain: float32 [2048], replicated, may hold values from 0.5 to 1.5
- w_query: bfloat16 [2048, 2048], P(None, 'tp')
- key_weight: bfloat16 [2048, 1024], P(None, 'tp')
- value_weight: bfloat16 [2048, 1024], P(None, 'tp'), may hold values from -0.125 to 0.125
- w_out: bfloat16 [2048, 2048], P('tp'), may hold values from -1 to 1
- query_gain: float32 [128], replicated, may hold values from 0.6 to 6, as said below
- key_gain: float32 [128], replicated, may hold values from 0.6 to 6, as said below
- seg_ids: int32 [16384], P('seq'), may hold values from 0 to 7, as said below
- positions: int32 [16384], P('seq'), may hold values from 0 to 13106, as said below
- post_gain: float32 [2048], replicated, may hold values from 0.5 to 1.5
- w_gate: bfloat16 [2048, 3072], P('seq', 'tp'), may hold values from -0.125 to 0.125
- w_up: bfloat16 [2048, 3072], P('seq', 'tp'), may hold values from -0.125 to 0.125
- w_down: bfloat16 [3072, 2048], P('tp', 'seq'), may hold values from -0.21875 to 0.21875
Outputs:
- hidden: bfloat16 [16384, 2048], P('seq')
- key_cache: bfloat16 [16384, 1024], P('seq', 'tp')
- value_cache: bfloat16 [16384, 1024], P('seq', 'tp')
Inputs may be any that keep to these rules, and one draw needn't show every extreme that they name: `seg_ids`: prompt numbers never fall along the stream; each of the 8 prompts is a contiguous run of one or more tokens, and one prompt has exactly 13107 tokens. `positions`: each token's place in its prompt, counting from 0 at the prompt's first token. `query_gain`: positive gains. `key_gain`: positive gains.
All inputs are finite; a program needn't handle non-finite values.
Results may differ from a plain program's by a relative error of at most 0.02.
Values may be sent and summed in bfloat16 or wider, within the bound.
A program may use at most 128 MiB of HBM per device.

v0:
```python
import math
import jax
import jax.numpy as jnp
from jax import lax
from jax.sharding import PartitionSpec as P


def rms(v, gain):
    return v * lax.rsqrt(jnp.mean(v * v, axis=-1, keepdims=True) + 1e-06) * gain


def rope(v, place):
    half = v.shape[-1] // 2
    freqs = 1000000.0 ** (-2.0 * jnp.arange(half, dtype=jnp.float32) / v.shape[-1])
    angle = place.astype(jnp.float32)[:, None] * freqs[None, :]
    cosine = jnp.cos(angle)[:, None, :]
    sine = jnp.sin(angle)[:, None, :]
    block_start = v[..., :half]
    second = v[..., half:]
    return jnp.concatenate(
        [block_start * cosine - second * sine, second * cosine + block_start * sine], axis=-1
    )


def body(
    layer_input,
    norm_gain,
    w_query,
    key_weight,
    value_weight,
    w_out,
    query_gain,
    key_gain,
    seg_ids,
    positions,
    post_gain,
    w_gate,
    w_up,
    w_down,
):
    rows = layer_input.shape[0]
    head_size = query_gain.shape[0]
    query_local = w_query.shape[1] // head_size
    kv_local = key_weight.shape[1] // head_size
    head_group = query_local // kv_local
    scale = 1.0 / math.sqrt(head_size)
    xf = layer_input.astype(jnp.float32)
    normed_input = rms(xf, norm_gain).astype(jnp.bfloat16)
    query_matrix = jnp.dot(normed_input, w_query, preferred_element_type=jnp.float32).reshape(
        rows, query_local, head_size
    )
    query_matrix = rope(rms(query_matrix, query_gain), positions).astype(jnp.bfloat16)
    key_matrix = jnp.dot(normed_input, key_weight, preferred_element_type=jnp.float32).reshape(
        rows, kv_local, head_size
    )
    key_matrix = rope(rms(key_matrix, key_gain), positions).astype(jnp.bfloat16)
    key_cache = key_matrix.reshape(rows, kv_local * head_size)
    value_cache = jnp.dot(normed_input, value_weight, preferred_element_type=jnp.float32).astype(
        jnp.bfloat16
    )
    grouped = query_matrix.reshape(rows, kv_local, head_group, head_size).transpose(1, 2, 0, 3)
    me = lax.axis_index("seq")
    my_last = me * rows + rows - 1

    def update(state, key_rows, value_rows, seg_rows, place_rows):
        top, total, acc = state
        count = key_rows.shape[0]
        s = (
            jnp.einsum(
                "hgqd,khd->hgqk",
                grouped,
                key_rows.reshape(count, kv_local, head_size),
                preferred_element_type=jnp.float32,
            )
            * scale
        )
        allowed = (seg_ids[:, None] == seg_rows[None, :]) & (
            place_rows[None, :] <= positions[:, None]
        )
        s = jnp.where(allowed, s, -1e30)
        new_top = jnp.maximum(top, jnp.max(s, axis=-1))
        p = jnp.where(allowed, jnp.exp(s - new_top[..., None]), 0.0)
        decay = jnp.exp(top - new_top)
        total = total * decay + jnp.sum(p, axis=-1)
        acc = acc * decay[..., None] + jnp.einsum(
            "hgqk,khd->hgqd",
            p.astype(jnp.bfloat16),
            value_rows.reshape(count, kv_local, head_size),
            preferred_element_type=jnp.float32,
        )
        return (new_top, total, acc)

    start_state = (
        jnp.full((kv_local, head_group, rows), -1e30, jnp.float32),
        jnp.zeros((kv_local, head_group, rows), jnp.float32),
        jnp.zeros((kv_local, head_group, rows, head_size), jnp.float32),
    )
    travel = (key_cache, value_cache, seg_ids, positions)
    dead = jnp.int32(0) < 0
    key_rows = lax.all_gather(travel[0], "seq", axis=0, tiled=True)
    value_rows = lax.all_gather(travel[1], "seq", axis=0, tiled=True)
    seg_rows = lax.all_gather(travel[2], "seq", axis=0, tiled=True)
    place_rows = lax.all_gather(travel[3], "seq", axis=0, tiled=True)
    count = key_rows.shape[0]
    shards = count // rows
    limit = max(1, 1024 // rows)
    factor = 1
    for trial in range(1, limit + 1):
        if shards % trial == 0:
            factor = trial
    width = rows * factor

    def one_block(step, inner):
        offset = step * width
        kb = lax.dynamic_slice_in_dim(key_rows, offset, width, 0)
        vb = lax.dynamic_slice_in_dim(value_rows, offset, width, 0)
        sb = lax.dynamic_slice_in_dim(seg_rows, offset, width, 0)
        pb = lax.dynamic_slice_in_dim(place_rows, offset, width, 0)
        skip = dead | (offset > my_last) | (sb[width - 1] < seg_ids[0])
        return lax.cond(skip, lambda c: c, lambda c: update(c, kb, vb, sb, pb), inner)

    top, total, acc = lax.fori_loop(0, count // width, one_block, start_state)
    attended = (acc / total[..., None]).astype(jnp.bfloat16)
    attended = attended.transpose(2, 0, 1, 3).reshape(rows, query_local * head_size)
    partial_out = jnp.dot(attended, w_out, preferred_element_type=jnp.float32)
    summed = lax.psum(partial_out.astype(jnp.bfloat16), "tp").astype(jnp.float32)
    mid = (xf + summed).astype(jnp.bfloat16)
    mid_f = mid.astype(jnp.float32)
    post_normed = rms(mid_f, post_gain).astype(jnp.bfloat16)
    gate = jnp.dot(
        post_normed,
        lax.all_gather(w_gate, "seq", axis=0, tiled=True),
        preferred_element_type=jnp.float32,
    )
    up = jnp.dot(
        post_normed,
        lax.all_gather(w_up, "seq", axis=0, tiled=True),
        preferred_element_type=jnp.float32,
    )
    act = (jax.nn.silu(gate) * up).astype(jnp.bfloat16)
    terms = jnp.dot(
        act, lax.all_gather(w_down, "seq", axis=1, tiled=True), preferred_element_type=jnp.float32
    )
    ffn_total = lax.psum(terms.astype(jnp.bfloat16), "tp").astype(jnp.float32)
    hidden = (mid_f + ffn_total).astype(jnp.bfloat16)
    return (hidden, key_cache, value_cache)


def solution(mesh):
    in_specs = (
        P("seq", None),
        P(),
        P(None, "tp"),
        P(None, "tp"),
        P(None, "tp"),
        P("tp", None),
        P(),
        P(),
        P("seq"),
        P("seq"),
        P(),
        P("seq", "tp"),
        P("seq", "tp"),
        P("tp", "seq"),
    )
    out_specs = (P("seq", None), P("seq", "tp"), P("seq", "tp"))
    return jax.shard_map(body, mesh=mesh, in_specs=in_specs, out_specs=out_specs, check_vma=False)
```

profile of v0, /device:TPU:2, one launch (start us, length us, event | category | flops | bytes accessed | tf_op | source)
XLA Modules:
  0.0 657.9 jit_solution(4688254087747547651)
XLA Ops:
  7.3 1.6 fusion.12
  8.9 3.0 multiply_reduce_fusion.1
  12.7 1.0 multiply_multiply_fusion.1
  13.8 0.8 copy.77
  14.6 2.4 convolution_convert_fusion.2
  17.1 3.2 fusion.28
  20.3 1.2 reshape.128
  22.8 46.4 %all-gather = s32[64,1,256]{2,1,0:T(1,128)S(1)} all-gather(s32[1,1,256]{2,1,0:T(1,128)S(1)} %bitcast.61), channel_id=1, replica_groups=mesh['seq'=64,'tp'=4] {'seq'}, dimensions={0}, use_global_device_ids=true | all-gather | bytes 66560 | tf_op jit(solution)/shard_map/all_gather | solution.py:102
  69.2 41.5 %all-gather.1 = s32[64,1,256]{2,1,0:T(1,128)S(1)} all-gather(s32[1,1,256]{2,1,0:T(1,128)S(1)} %bitcast.60), channel_id=1, replica_groups=mesh['seq'=64,'tp'=4] {'seq'}, dimensions={0}, use_global_device_ids=true | all-gather | bytes 66560 | tf_op jit(solution)/shard_map/all_gather | solution.py:103
  110.9 11.9 %copy.67 = bf16[16384,256]{0,1:T(8,128)(2,1)} copy(bf16[16384,256]{1,0:T(8,128)(2,1)} %all-gather.8.cloned.1.call-done) | data formatting | bytes 16777216 | tf_op jit(solution)/shard_map/while | solution.py:122
  122.8 60.4 %all-gather.10.cloned.1.call-done = bf16[16384,256]{1,0:T(8,128)(2,1)} async-done(((bf16[256,256]{1,0:T(8,128)(2,1)}), bf16[16384,256]{1,0:T(8,128)(2,1)}) %all-gather.10.cloned.1.call-update) | async-done | bytes 8388624 | tf_op jit(solution)/shard_map/all_gather | solution.py:101
  183.2 11.8 %copy.68 = bf16[16384,256]{0,1:T(8,128)(2,1)} copy(bf16[16384,256]{1,0:T(8,128)(2,1)} %all-gather.10.cloned.1.call-done) | data formatting | bytes 16777216 | tf_op jit(solution)/shard_map/while | solution.py:122
  195.0 44.5 %while.17 = (s32[]{:T(128)}, f32[2,2,256]{2,1,0:T(2,128)S(1)}, f32[2,2,256]{2,1,0:T(2,128)S(1)}, f32[2,2,256,128]{3,2,1,0:T(8,128)S(1)}, s32[]{:T(128)}, /*index...) while((s32[]{:T(128)}, f32[2,2,256]{2,1,0:T(2,128)S(1)}, ...), condition=%wide.region_8.9_spmd, body=%wide.region_3.8_spmd.sunk | while | flops 551553024 | bytes 18180480 | solution.py:122
  197.4 5.3 conditional.2
  197.8 1.3 constant_dynamic-slice_fusion
  199.1 0.9 fusion
  200.0 1.0 fusion.2
  201.1 1.6 fusion.6
  205.2 0.6 slice.44
  207.7 0.6 slice.44
  215.1 0.6 slice.44
  217.5 0.6 slice.44
  239.8 1.7 convolution_convert_fusion
  243.5 110.3 %all-reduce.3.cloned.1.call-done = bf16[256,2048]{1,0:T(8,128)(2,1)} async-done(((bf16[256,2048]{1,0:T(8,128)(2,1)}), bf16[256,2048]{1,0:T(8,128)(2,1)}) %all-reduce.3.cloned.1.call-update) | async-done | bytes 1048592 | tf_op jit(solution)/shard_map/psum | solution.py:126
  353.8 2.0 fusion.16
  355.9 78.9 %all-gather.12.cloned.1.call-done = bf16[2048,768]{1,0:T(8,128)(2,1)} async-done(((bf16[32,768]{1,0:T(8,128)(2,1)}), bf16[2048,768]{1,0:T(8,128)(2,1)}) %all-gather.12.cloned.1.call-update) | async-done | bytes 3145744 | tf_op jit(solution)/shard_map/all_gather | solution.py:132
  434.8 3.8 fusion.24
  438.6 75.0 %all-gather.14.cloned.1.call-done = bf16[2048,768]{1,0:T(8,128)(2,1)} async-done(((bf16[32,768]{1,0:T(8,128)(2,1)}), bf16[2048,768]{1,0:T(8,128)(2,1)}) %all-gather.14.cloned.1.call-update) | async-done | bytes 3145744 | tf_op jit(solution)/shard_map/all_gather | solution.py:137
  513.6 78.8 %all-gather.16.cloned.1.call-done = bf16[768,2048]{0,1:T(8,128)(2,1)} async-done(((bf16[768,32]{0,1:T(8,128)(2,1)}), bf16[768,2048]{0,1:T(8,128)(2,1)}) %all-gather.16.cloned.1.call-update) | async-done | bytes 3145744 | tf_op jit(solution)/shard_map/all_gather | solution.py:142
  592.4 6.2 convolution_convert_fusion.1
  598.7 49.8 %all-reduce.5.cloned.1.call-done = bf16[256,2048]{1,0:T(8,128)(2,1)} async-done(((bf16[256,2048]{1,0:T(8,128)(2,1)}), bf16[256,2048]{1,0:T(8,128)(2,1)}) %all-reduce.5.cloned.1.call-update) | async-done | bytes 1048592 | tf_op jit(solution)/shard_map/psum | solution.py:144
  648.5 2.6 fusion.19
  (145 shorter events, 21.2 us)
Async XLA Ops:
  7.2 232.6 %copy-start = (bf16[512,2048]{1,0:T(8,128)(2,1)S(1)}, bf16[512,2048]{1,0:T(8,128)(2,1)}, u32[]{:S(2)}) copy-start(bf16[512,2048]{1,0:T(8,128)(2,1)} %param.23) | copy-start | bytes 6291460
  7.2 4.8 copy-start.2
  7.2 103.7 %all-gather.8.cloned.1.call-start = ((), (), s32[]{:S(2)}) async-start(), calls=%async_computation | async-start | bytes 8519680 | tf_op jit(solution)/shard_map/all_gather | solution.py:100
  8.9 3.8 copy-start.4
  8.9 5.7 copy-start.1
  14.6 168.6 %all-gather.10.cloned.1.call-start = ((), (), s32[]{:S(2)}) async-start(), calls=%async_computation.1 | async-start | bytes 8519680 | tf_op jit(solution)/shard_map/all_gather | solution.py:101
  17.0 336.8 %all-reduce.3.cloned.1.call-start = ((), (), s32[]{:S(2)}) async-start(), calls=%async_computation.2 | async-start | bytes 2097152 | tf_op jit(solution)/shard_map/psum | solution.py:126
  17.1 4.8 copy-start.5
  21.9 1.0 copy-start.3
  241.5 193.3 %copy-start.6 = (f32[2048]{0:T(1024)S(1)}, f32[2048]{0:T(1024)}, u32[]{:S(2)}) copy-start(f32[2048]{0:T(1024)} %param.28) | copy-start | bytes 24580
  241.5 193.3 %all-gather.12.cloned.1.call-start = ((), (), s32[]{:S(2)}) async-start(), calls=%async_computation.3 | async-start | bytes 3194880 | tf_op jit(solution)/shard_map/all_gather | solution.py:132
  242.1 271.5 %all-gather.14.cloned.1.call-start = ((), (), s32[]{:S(2)}) async-start(), calls=%async_computation.4 | async-start | bytes 3194880 | tf_op jit(solution)/shard_map/all_gather | solution.py:137
  242.7 349.7 %all-gather.16.cloned.1.call-start = ((), (), s32[]{:S(2)}) async-start(), calls=%async_computation.5 | async-start | bytes 3194880 | tf_op jit(solution)/shard_map/all_gather | solution.py:142
  243.3 405.2 %all-reduce.5.cloned.1.call-start = ((), (), s32[]{:S(2)}) async-start(), calls=%async_computation.6 | async-start | bytes 2097152 | tf_op jit(solution)/shard_map/psum | solution.py:144
Sparse Core Ops, SparseCore 0:
  14.7 84.7 all-gather.7
  102.8 80.3 all-gather.9
  241.7 112.1 all-reduce.2
  356.8 77.9 all-gather.11
  437.8 75.7 all-gather.13
  516.6 75.7 all-gather.15
  598.8 49.6 all-reduce.4
where the time goes:
time: 659 us; the launch traced here: 658 us
  waiting for transfers between devices  455 us (69%)
  blocking collectives  87.9 us (13%)
  local copies, waits for them, and re-layouts  45.7 us (7%)
  matrix products  22.9 us (3%)
  loops' own time  21 us (3%)
  between operations  14.4 us (2%)
  other arithmetic  10.7 us (2%)
    psum x1, waiting for transfers between devices, body(): lax.psum(partial_out.astype(jnp.bfloat16), 'tp').astype(jnp.float32)  110 us
    all_gather x1, waiting for transfers between devices, body(): lax.all_gather(w_gate, 'seq', axis=0, tiled=True)  78.9 us
    all_gather x1, waiting for transfers between devices, body(): lax.all_gather(w_down, 'seq', axis=1, tiled=True)  78.8 us
    all_gather x1, waiting for transfers between devices, body(): lax.all_gather(w_up, 'seq', axis=0, tiled=True)  75 us
    all_gather x1, waiting for transfers between devices, body(): value_rows = lax.all_gather(travel[1], 'seq', axis=0, tiled=True)  60.4 us
    psum x1, waiting for transfers between devices, body(): ffn_total = lax.psum(terms.astype(jnp.bfloat16), 'tp').astype(jnp.float32)  49.8 us
    all_gather x1, blocking collectives, body(): seg_rows = lax.all_gather(travel[2], 'seq', axis=0, tiled=True)  46.4 us
    all_gather x1, blocking collectives, body(): place_rows = lax.all_gather(travel[3], 'seq', axis=0, tiled=True)  41.5 us
  transfers between devices with their start and end apart: 7, of which 6 were waited for; matrix products, arithmetic and copies ran while one was open for 4% of the time, Pallas kernels for 0%

commit v1 on v0

--- a/solution.py
+++ b/solution.py
@@ -98,7 +98,9 @@
     travel = (key_cache, value_cache, seg_ids, positions)
     dead = jnp.int32(0) < 0
     key_rows = lax.all_gather(travel[0], "seq", axis=0, tiled=True)
-    value_rows = lax.all_gather(travel[1], "seq", axis=0, tiled=True)
+    value_rows = jnp.concatenate(
+        lax.all_to_all(jnp.stack([travel[1]] * lax.axis_size("seq")), "seq", 0, 0), axis=0
+    )
     seg_rows = lax.all_gather(travel[2], "seq", axis=0, tiled=True)
     place_rows = lax.all_gather(travel[3], "seq", axis=0, tiled=True)
     count = key_rows.shape[0]

time: 659 us -> 811 us (1.23)
  blocking collectives: 87.9 us -> 274 us
  waiting for transfers between devices: 455 us -> 395 us
  local copies, waits for them, and re-layouts: 45.7 us -> 61.5 us
  starting transfers between devices: 0.46 us -> 12.6 us
    all_gather x1, blocking collectives: 46.4 us -> 232 us  [body(): seg_rows = lax.all_gather(travel[2], 'seq', axis=0, tiled=True)]
    all_gather x1 -> x0, waiting for transfers between devices: 60.4 us -> none  [body(): value_rows = lax.all_gather(travel[1], 'seq', axis=0, tiled=True)]
    all_to_all x0 -> x1, starting transfers between devices: none -> 12.3 us  [body(): lax.all_to_all(jnp.stack([travel[1]] * lax.axis_size('seq')), 'seq', 0, 0)]
    all_to_all x0 -> x1, local copies, waits for them, and re-layouts: none -> 11.6 us  [body(): lax.all_to_all(jnp.stack([travel[1]] * lax.axis_size('seq')), 'seq', 0, 0)]
  transfers between devices with their start and end apart: 7 -> 7, of which waited for: 6 -> 5; matrix products, arithmetic and copies ran while one was open for 4% -> 5% of each run, Pallas kernels for 0% -> 0%
where the time goes in v1:
time: 811 us; the launch traced here: 809 us
  waiting for transfers between devices  395 us (49%)
  blocking collectives  274 us (34%)
  local copies, waits for them, and re-layouts  61.5 us (8%)
  matrix products  22.1 us (3%)
  loops' own time  19.2 us (2%)
  between operations  14.4 us (2%)
  starting transfers between devices  12.6 us (2%)
  other arithmetic  10.8 us (1%)
    all_gather x1, blocking collectives, body(): seg_rows = lax.all_gather(travel[2], 'seq', axis=0, tiled=True)  232 us
    psum x1, waiting for transfers between devices, body(): lax.psum(partial_out.astype(jnp.bfloat16), 'tp').astype(jnp.float32)  110 us
    all_gather x1, waiting for transfers between devices, body(): lax.all_gather(w_gate, 'seq', axis=0, tiled=True)  79.1 us
    all_gather x1, waiting for transfers between devices, body(): lax.all_gather(w_down, 'seq', axis=1, tiled=True)  78.8 us
    all_gather x1, waiting for transfers between devices, body(): lax.all_gather(w_up, 'seq', axis=0, tiled=True)  75 us
    psum x1, waiting for transfers between devices, body(): ffn_total = lax.psum(terms.astype(jnp.bfloat16), 'tp').astype(jnp.float32)  49.8 us
    all_gather x1, blocking collectives, body(): place_rows = lax.all_gather(travel[3], 'seq', axis=0, tiled=True)  41.7 us
    while x3, local copies, waits for them, and re-layouts, body(): top, total, acc = lax.fori_loop(0, count // width, one_block, start_state)  24.1 us
  transfers between devices with their start and end apart: 7, of which 5 were waited for; matrix products, arithmetic and copies ran while one was open for 5% of the time, Pallas kernels for 0%

profile of v1, /device:TPU:2, one launch (start us, length us, event | category | flops | bytes accessed | tf_op | source)
XLA Modules:
  0.0 809.1 jit_solution(17409629084696459028)
XLA Ops:
  7.2 1.7 fusion.12
  8.8 2.1 convolution_convert_fusion.2
  11.6 4.3 stack.2
  15.8 12.3 %all-to-all-start = ((bf16[64,256,256]{1,2,0:T(8,128)(2,1)}), bf16[64,256,256]{1,2,0:T(8,128)(2,1)}, u32[]{:S(2)}, u32[]{:S(2)}) async-start(bf16[64,256,256]{1,2,0:T(8,128)(2,1)} %stack.2), calls=%async_computation | async-start | bytes 16777216 | tf_op jit(solution)/shard_map/all_to_all | solution.py:102
  28.3 2.6 multiply_reduce_fusion.1
  31.6 1.0 multiply_multiply_fusion.1
  32.7 0.8 copy.94
  33.6 3.2 fusion.28
  36.7 1.2 reshape.133
  39.3 232.2 %all-gather = s32[64,1,256]{2,1,0:T(1,128)S(1)} all-gather(s32[1,1,256]{2,1,0:T(1,128)S(1)} %bitcast.63), channel_id=1, replica_groups=mesh['seq'=64,'tp'=4] {'seq'}, dimensions={0}, use_global_device_ids=true | all-gather | bytes 66560 | tf_op jit(solution)/shard_map/all_gather | solution.py:104
  271.5 41.7 %all-gather.1 = s32[64,1,256]{2,1,0:T(1,128)S(1)} all-gather(s32[1,1,256]{2,1,0:T(1,128)S(1)} %bitcast.62), channel_id=1, replica_groups=mesh['seq'=64,'tp'=4] {'seq'}, dimensions={0}, use_global_device_ids=true | all-gather | bytes 66560 | tf_op jit(solution)/shard_map/all_gather | solution.py:105
  313.4 11.6 %copy.83 = bf16[64,256,256]{2,1,0:T(8,128)(2,1)} copy(bf16[64,256,256]{1,2,0:T(8,128)(2,1)} %all-to-all-done) | data formatting | bytes 16777216 | tf_op jit(solution)/shard_map/all_to_all | solution.py:102
  325.0 12.0 %copy.85 = bf16[16384,256]{0,1:T(8,128)(2,1)} copy(bf16[16384,256]{1,0:T(8,128)(2,1)} %bitcast.54) | data formatting | bytes 16777216 | tf_op jit(solution)/shard_map/while | solution.py:124
  336.9 12.0 %copy.84 = bf16[16384,256]{0,1:T(8,128)(2,1)} copy(bf16[16384,256]{1,0:T(8,128)(2,1)} %all-gather.7.cloned.1.call-done) | data formatting | bytes 16777216 | tf_op jit(solution)/shard_map/while | solution.py:124
  349.0 41.7 %while.17 = (s32[]{:T(128)}, f32[2,2,256]{2,1,0:T(2,128)S(1)}, f32[2,2,256]{2,1,0:T(2,128)S(1)}, f32[2,2,256,128]{3,2,1,0:T(8,128)S(1)}, s32[]{:T(128)}, /*index...) while((s32[]{:T(128)}, f32[2,2,256]{2,1,0:T(2,128)S(1)}, ...), condition=%wide.region_8.9_spmd, body=%wide.region_3.8_spmd.sunk | while | flops 551553024 | bytes 18180480 | solution.py:124
  349.0 0.6 slice.44
  351.2 5.3 conditional.2
  351.6 1.3 constant_dynamic-slice_fusion
  352.9 0.9 fusion
  353.8 1.0 fusion.2
  354.9 1.6 fusion.6
  391.0 1.7 convolution_convert_fusion
  392.7 0.7 all-gather.9.cloned.1.call-update
  394.6 110.3 %all-reduce.3.cloned.1.call-done = bf16[256,2048]{1,0:T(8,128)(2,1)} async-done(((bf16[256,2048]{1,0:T(8,128)(2,1)}), bf16[256,2048]{1,0:T(8,128)(2,1)}) %all-reduce.3.cloned.1.call-update) | async-done | bytes 1048592 | tf_op jit(solution)/shard_map/psum | solution.py:128
  504.9 2.0 fusion.16
  506.9 79.1 %all-gather.9.cloned.1.call-done = bf16[2048,768]{1,0:T(8,128)(2,1)} async-done(((bf16[32,768]{1,0:T(8,128)(2,1)}), bf16[2048,768]{1,0:T(8,128)(2,1)}) %all-gather.9.cloned.1.call-update) | async-done | bytes 3145744 | tf_op jit(solution)/shard_map/all_gather | solution.py:134
  586.0 3.8 fusion.24
  589.8 75.0 %all-gather.11.cloned.1.call-done = bf16[2048,768]{1,0:T(8,128)(2,1)} async-done(((bf16[32,768]{1,0:T(8,128)(2,1)}), bf16[2048,768]{1,0:T(8,128)(2,1)}) %all-gather.11.cloned.1.call-update) | async-done | bytes 3145744 | tf_op jit(solution)/shard_map/all_gather | solution.py:139
  664.8 78.8 %all-gather.13.cloned.1.call-done = bf16[768,2048]{0,1:T(8,128)(2,1)} async-done(((bf16[768,32]{0,1:T(8,128)(2,1)}), bf16[768,2048]{0,1:T(8,128)(2,1)}) %all-gather.13.cloned.1.call-update) | async-done | bytes 3145744 | tf_op jit(solution)/shard_map/all_gather | solution.py:144
  743.6 6.2 convolution_convert_fusion.1
  749.9 49.8 %all-reduce.5.cloned.1.call-done = bf16[256,2048]{1,0:T(8,128)(2,1)} async-done(((bf16[256,2048]{1,0:T(8,128)(2,1)}), bf16[256,2048]{1,0:T(8,128)(2,1)}) %all-reduce.5.cloned.1.call-update) | async-done | bytes 1048592 | tf_op jit(solution)/shard_map/psum | solution.py:146
  799.7 2.6 fusion.19
  (151 shorter events, 22.1 us)
Async XLA Ops:
  7.2 383.8 %copy-start = (bf16[512,2048]{1,0:T(8,128)(2,1)S(1)}, bf16[512,2048]{1,0:T(8,128)(2,1)}, u32[]{:S(2)}) copy-start(bf16[512,2048]{1,0:T(8,128)(2,1)} %param.23) | copy-start | bytes 6291460
  10.9 0.7 copy-start.2
  15.8 12.4 %copy-start.1 = (bf16[256,2048]{1,0:T(8,128)(2,1)S(1)}, bf16[256,2048]{1,0:T(8,128)(2,1)}, u32[]{:S(2)}) copy-start(bf16[256,2048]{1,0:T(8,128)(2,1)} %param.18) | copy-start | bytes 3145732
  15.8 12.4 %copy-start.7 = (f32[2048]{0:T(1024)S(1)}, f32[2048]{0:T(1024)}, u32[]{:S(2)}) copy-start(f32[2048]{0:T(1024)} %param.19) | copy-start | bytes 24580
  15.8 15.0 %copy-start.3 = (s32[256]{0:T(256)S(1)}, s32[256]{0:T(256)}, u32[]{:S(2)}) copy-start(s32[256]{0:T(256)} %param.27) | copy-start | bytes 3076
  15.8 297.5 %all-to-all-start = ((bf16[64,256,256]{1,2,0:T(8,128)(2,1)}), bf16[64,256,256]{1,2,0:T(8,128)(2,1)}, u32[]{:S(2)}, u32[]{:S(2)}) async-start(bf16[64,256,256]{1,2,0:T(8,128)(2,1)} %stack.2), calls=%async_computation | async-start | bytes 16777216 | tf_op jit(solution)/shard_map/all_to_all | solution.py:102
  28.2 3.4 copy-start.5
  28.2 308.7 %all-gather.7.cloned.1.call-start = ((), (), s32[]{:S(2)}) async-start(), calls=%async_computation.1 | async-start | bytes 8519680 | tf_op jit(solution)/shard_map/all_gather | solution.py:100
  33.5 471.4 %all-reduce.3.cloned.1.call-start = ((), (), s32[]{:S(2)}) async-start(), calls=%async_computation.2 | async-start | bytes 2097152 | tf_op jit(solution)/shard_map/psum | solution.py:128
  33.5 4.8 copy-start.6
  36.7 2.6 copy-start.4
  390.9 195.1 %copy-start.8 = (f32[2048]{0:T(1024)S(1)}, f32[2048]{0:T(1024)}, u32[]{:S(2)}) copy-start(f32[2048]{0:T(1024)} %param.28) | copy-start | bytes 24580
  392.7 193.3 %all-gather.9.cloned.1.call-start = ((), (), s32[]{:S(2)}) async-start(), calls=%async_computation.3 | async-start | bytes 3194880 | tf_op jit(solution)/shard_map/all_gather | solution.py:134
  393.4 271.4 %all-gather.11.cloned.1.call-start = ((), (), s32[]{:S(2)}) async-start(), calls=%async_computation.4 | async-start | bytes 3194880 | tf_op jit(solution)/shard_map/all_gather | solution.py:139
  394.0 349.6 %all-gather.13.cloned.1.call-start = ((), (), s32[]{:S(2)}) async-start(), calls=%async_computation.5 | async-start | bytes 3194880 | tf_op jit(solution)/shard_map/all_gather | solution.py:144
  394.6 405.1 %all-reduce.5.cloned.1.call-start = ((), (), s32[]{:S(2)}) async-start(), calls=%async_computation.6 | async-start | bytes 2097152 | tf_op jit(solution)/shard_map/psum | solution.py:146
Sparse Core Ops, SparseCore 0:
  33.6 146.4 all-gather.6
  392.8 112.0 all-reduce.2
  508.0 77.9 all-gather.8
  589.0 75.7 all-gather.10
  667.8 75.7 all-gather.12
  750.0 49.6 all-reduce.4
